TPU v7x, 32 devices: a whole 2x2x4 slice. The times are simulated.
32 devices in a mesh: member: 2 (over x), ty: 16 (over z, y, core).
Axes of the slice: x: 2, y: 2, z: 4, core: 2. Of those that a mesh axis runs over, the one named last changes fastest.
Arguments:
- fields: float32 [32, 768, 6, 768], P('member', 'ty'), parts along dimension 0, may hold values from -6 to 6
- damp_four: float32 [32], P('member'), parts along dimension 0, may hold values from 0.004 to 0.03
- damp_six: float32 [32], P('member'), parts along dimension 0, may hold values from 0.0008 to 0.006
- metric: float32 [4, 768, 6, 768], P(None, 'ty'), may hold values from 0.1 to 1.9
- seam_table: int32 [6, 4, 3], replicated, may hold values from 0 to 5
Outputs:
- damped: float32 [32, 768, 6, 768], P('member', 'ty'), parts along dimension 0
There are 2 independent parts, one for each index of `member`. A program takes and returns all parts, laid end to end along the dimension named above; an argument that names none is the same for every part. Nothing has to cross between parts.
Inputs may be any that keep to these rules, and one draw needn't show every extreme that they name: The table describes the surface of a cube with every face seen from outside: the joining is symmetric, no face is joined to itself, and r is 1 exactly when both edges are among (south, east) or both among (north, west).
All inputs are finite; a program needn't handle non-finite values.
Results may differ from a plain program's by a relative error of at most 0.00005.
Values sent between devices are 32-bit elements; how exact they have to be, the bound alone decides.
A program may use at most 128 MiB of HBM per device.

v0:
```python
import jax
import jax.numpy as jnp
from jax import lax
from jax.sharding import PartitionSpec as P


def with_halo(cells, sides, width):
    for axis, dim in sides:
        count = lax.axis_size(axis)
        ends = count - 1
        head = lax.slice_in_dim(cells, 0, width, axis=dim)
        tail = lax.slice_in_dim(cells, cells.shape[dim] - width, cells.shape[dim], axis=dim)
        cells = jnp.concatenate(
            [
                lax.ppermute(tail, axis, [(i, (i + 1) % count) for i in range(ends)]),
                cells,
                lax.ppermute(head, axis, [((i + 1) % count, i) for i in range(ends)]),
            ],
            axis=dim,
        )
    return cells


def strip_edges(source):
    east_cells = jnp.transpose(source[:, :, :, -1], (0, 2, 1))
    west_cells = jnp.transpose(source[:, :, :, 0], (0, 2, 1))
    return jnp.stack([east_cells, west_cells], axis=2)


def gather_edges(source):
    tile_index = lax.axis_index("ty")
    tile_count = lax.axis_size("ty")
    strip_rows = source.shape[1]
    row_width = source.shape[3]
    strip_cells = strip_edges(source)
    first_row = jnp.where(tile_index == 0, source[:, 0], 0.0)
    last_row = jnp.where(tile_index == tile_count - 1, source[:, -1], 0.0)
    blank = jnp.zeros(strip_cells.shape[:3] + (row_width,), jnp.float32)
    placed = lax.dynamic_update_slice_in_dim(blank, strip_cells, tile_index * strip_rows, 3)
    rim_cells = jnp.stack([first_row, placed[:, :, 0], last_row, placed[:, :, 1]], axis=2)
    edge_set = lax.psum(rim_cells, "ty")
    return edge_set


def seam_halo(edge_set, seam_table):
    levels = edge_set.shape[0]
    row_width = edge_set.shape[3]
    flattened = edge_set.reshape(levels, 24, row_width)
    picked = (seam_table[:, :, 0] * 4 + seam_table[:, :, 1]).reshape(24)
    onehot = (picked[:, None] == jnp.arange(24, dtype=jnp.int32)[None, :]).astype(jnp.float32)
    neighbor = jnp.einsum("jk,lkc->ljc", onehot, flattened, precision=lax.Precision.HIGHEST)
    neighbor = neighbor.reshape(levels, 6, 4, row_width)
    flipped = (seam_table[:, :, 2] == 1)[None, :, :, None]
    return jnp.where(flipped, neighbor[..., ::-1], neighbor)


def laplace(source, metric, seam_table):
    tile_index = lax.axis_index("ty")
    tile_count = lax.axis_size("ty")
    strip_rows = source.shape[1]
    padded = with_halo(source, (("ty", 1),), 1)
    halo_cells = seam_halo(gather_edges(source), seam_table)
    south_row = jnp.where(tile_index == 0, halo_cells[:, :, 0], padded[:, 0])
    north_row = jnp.where(tile_index == tile_count - 1, halo_cells[:, :, 2], padded[:, -1])
    row_start = tile_index * strip_rows
    west_cells = jnp.transpose(
        lax.dynamic_slice_in_dim(halo_cells[:, :, 3], row_start, strip_rows, 2), (0, 2, 1)
    )[..., None]
    east_cells = jnp.transpose(
        lax.dynamic_slice_in_dim(halo_cells[:, :, 1], row_start, strip_rows, 2), (0, 2, 1)
    )[..., None]
    padded_x = jnp.concatenate([west_cells, source, east_cells], axis=3)
    padded_y = jnp.concatenate([south_row[:, None], source, north_row[:, None]], axis=1)
    return (
        metric[0] * (padded_x[..., :-2] - source)
        + metric[1] * (padded_x[..., 2:] - source)
        + metric[2] * (padded_y[:, :-2] - source)
        + metric[3] * (padded_y[:, 2:] - source)
    )


def per_device(fields, damp_four, damp_six, metric, seam_table):
    second = laplace(fields, metric, seam_table)
    fourth = laplace(second, metric, seam_table)
    sixth = laplace(fourth, metric, seam_table)
    return fields - damp_four[:, None, None, None] * fourth + damp_six[:, None, None, None] * sixth


def solution(mesh):
    placed = (
        P("member", "ty", None, None),
        P("member"),
        P("member"),
        P(None, "ty", None, None),
        P(),
    )
    return jax.shard_map(
        per_device,
        mesh=mesh,
        in_specs=placed,
        out_specs=P("member", "ty", None, None),
        check_vma=False,
    )
```

profile of v0, /device:TPU:0, one launch (start us, length us, event | category | flops | bytes accessed | tf_op | source)
XLA Modules:
  0.0 596.8 jit_solution(6882728278029485408)
XLA Ops:
  6.5 4.6 fusion.54
  11.1 18.5 %copy.89 = f32[16,48,6,768]{3,0,2,1:T(8,128)} copy(f32[16,48,6,768]{3,1,2,0:T(8,128)} %param.5) | data formatting | bytes 28311552 | tf_op args[0]
  38.1 4.7 collective-permute-start
  49.8 88.0 %all-reduce.4.cloned.1.call-done = f32[16,24,768]{2,1,0:T(8,128)} async-done(((f32[16,24,768]{2,1,0:T(8,128)}), f32[16,24,768]{2,1,0:T(8,128)}) %all-reduce.4.cloned.1.call-update) | async-done | bytes 1179664 | tf_op jit(solution)/shard_map/psum | solution.py:41
  141.1 4.7 rev.9
  150.1 3.9 copy.68
  155.7 4.0 copy.73
  161.7 33.4 %fusion.26 = f32[16,48,6,768]{3,0,2,1:T(8,128)} fusion(f32[16,48,6,768]{3,0,2,1:T(8,128)} %copy.89, f32[16,1,6,768]{3,0,2,1:T(8,128)} %get-tuple-element.38, f32[16,1,6,768]{3,0,2,1:T(8,128)} %get-tuple-element.37, f32[16,48,6,1]{3,0,2,1:T(8,128)} %copy.73, f32[16,48,6,1]{3,0,2,1:T(8,128)} %copy.68, f32[48,6,768]{2,1,0:T(8,128)} %copy.79, ...), kind=kLoop, calls=%fused_computation.35 | loop fusion | flops 53084160 | bytes 32477184 | tf_op jit(solution)/shard_map/add | solution.py:75
  195.1 5.3 fusion.52
  202.5 3.4 copy.104
  205.9 3.4 copy.83
  220.1 3.2 collective-permute-start.2
  224.6 91.8 %all-reduce.6.cloned.1.call-done = f32[16,24,768]{2,1,0:T(8,128)} async-done(((f32[16,24,768]{2,1,0:T(8,128)}), f32[16,24,768]{2,1,0:T(8,128)}) %all-reduce.6.cloned.1.call-update) | async-done | bytes 1179664 | tf_op jit(solution)/shard_map/psum | solution.py:41
  316.4 3.0 convolution_bitcast_fusion.1
  319.3 10.9 %reshape.133 = f32[16,6,4,768]{3,2,1,0:T(4,128)} reshape(f32[16,24,768]{2,1,0:T(8,128)} %convolution_bitcast_fusion.1) | data formatting | bytes 2359296 | tf_op jit(solution)/shard_map/reshape | solution.py:52
  330.3 2.7 copy.85
  332.9 4.7 rev.10
  342.1 3.9 copy.87
  347.7 4.0 copy.88
  353.7 34.7 %fusion.15 = f32[16,48,6,768]{3,0,2,1:T(8,128)} fusion(f32[16,48,6,768]{3,0,2,1:T(8,128)} %fusion.26, f32[16,1,6,768]{3,0,2,1:T(8,128)} %get-tuple-element.34, f32[16,1,6,768]{3,0,2,1:T(8,128)} %get-tuple-element.33, f32[16,48,6,1]{3,0,2,1:T(8,128)} %copy.88, f32[16,48,6,1]{3,0,2,1:T(8,128)} %copy.87, f32[48,6,768]{2,1,0:T(8,128)} %copy.79, ...), kind=kLoop, calls=%fused_computation.20 | loop fusion | flops 53084160 | bytes 32477184 | tf_op jit(solution)/shard_map/add | solution.py:75
  388.4 5.3 fusion.50
  395.8 3.4 copy.90
  399.2 3.4 copy.91
  410.7 2.8 reshape.134
  413.6 3.2 collective-permute-start.4
  418.1 91.7 %all-reduce.8.cloned.1.call-done = f32[16,24,768]{2,1,0:T(8,128)} async-done(((f32[16,24,768]{2,1,0:T(8,128)}), f32[16,24,768]{2,1,0:T(8,128)}) %all-reduce.8.cloned.1.call-update) | async-done | bytes 1179664 | tf_op jit(solution)/shard_map/psum | solution.py:41
  509.8 3.0 convolution_bitcast_fusion
  518.0 4.7 rev.11
  526.5 3.9 copy.97
  530.5 4.0 copy.98
  536.0 35.3 %fusion.4 = f32[16,48,6,768]{3,0,2,1:T(8,128)} fusion(f32[16,48,6,768]{3,0,2,1:T(8,128)} %fusion.15, f32[16,1,6,768]{3,0,2,1:T(8,128)S(1)} %get-tuple-element.30, f32[16,1,6,768]{3,0,2,1:T(8,128)S(1)} %get-tuple-element.29, f32[16,48,6,1]{3,0,2,1:T(8,128)} %copy.98, f32[16,48,6,1]{3,0,2,1:T(8,128)} %copy.97, f32[16]{0:T(128)S(1)} %copy-done.5, ...), kind=kLoop, calls=%fused_computation.5 | loop fusion | flops 67239936 | bytes 46633088 | tf_op jit(solution)/shard_map/add | solution.py:86
  571.3 18.5 %copy.99 = f32[16,48,6,768]{3,1,2,0:T(8,128)} copy(f32[16,48,6,768]{3,0,2,1:T(8,128)} %fusion.4) | data formatting | bytes 28311552 | tf_op jit(solution)/shard_map/add | solution.py:86
  (83 shorter events, 70.8 us)
Async XLA Ops:
  6.5 131.3 %all-reduce.4.cloned.1.call-start = ((), (), s32[]{:S(2)}) async-start(), calls=%async_computation | async-start | bytes 2359296 | tf_op jit(solution)/shard_map/psum | solution.py:41
  36.6 7.5 %copy-start.4 = (s32[6,4,3]{0,1,2:T(4,128)S(1)}, s32[6,4,3]{0,1,2:T(4,128)}, u32[]{:S(2)}) copy-start(s32[6,4,3]{0,1,2:T(4,128)} %param.9) | copy-start | bytes 868
  38.0 278.3 %all-reduce.6.cloned.1.call-start = ((), (), s32[]{:S(2)}) async-start(), calls=%async_computation.1 | async-start | bytes 2359296 | tf_op jit(solution)/shard_map/psum | solution.py:41
  38.1 121.6 %collective-permute-start = (f32[16,1,6,768]{3,0,2,1:T(8,128)}, f32[16,1,6,768]{3,0,2,1:T(8,128)}, u32[]{:S(2)}, u32[]{:S(2)}) collective-permute-start(f32[16,1,6,768]{3,0,2,1:T(8,128)} %get-tuple-element.17), channel_id=1, source_target_pairs={{0,1},{1,2},{2,3},{3,4},{4,5},{5,6},{6,7},{7,8},{8,9},{9,10},{10,1... | collective-permute-start | bytes 884744 | tf_op jit(solution)/shard_map/ppermute | solution.py:15
  42.8 116.8 %collective-permute-start.1 = (f32[16,1,6,768]{3,0,2,1:T(8,128)}, f32[16,1,6,768]{3,0,2,1:T(8,128)}, u32[]{:S(2)}, u32[]{:S(2)}) collective-permute-start(f32[16,1,6,768]{3,0,2,1:T(8,128)} %get-tuple-element.19), channel_id=1, source_target_pairs={{1,0},{2,1},{3,2},{4,3},{5,4},{6,5},{7,6},{8,7},{9,8},{10,9},{11,1... | collective-permute-start | bytes 884744 | tf_op jit(solution)/shard_map/ppermute | solution.py:17
  147.7 1.0 copy-start.2
  220.0 289.8 %all-reduce.8.cloned.1.call-start = ((), (), s32[]{:S(2)}) async-start(), calls=%async_computation.2 | async-start | bytes 2359296 | tf_op jit(solution)/shard_map/psum | solution.py:41
  220.1 131.6 %collective-permute-start.2 = (f32[16,1,6,768]{3,0,2,1:T(8,128)}, f32[16,1,6,768]{3,0,2,1:T(8,128)}, u32[]{:S(2)}, u32[]{:S(2)}) collective-permute-start(f32[16,1,6,768]{3,0,2,1:T(8,128)} %get-tuple-element.11), channel_id=1, source_target_pairs={{0,1},{1,2},{2,3},{3,4},{4,5},{5,6},{6,7},{7,8},{8,9},{9,10},{10,1... | collective-permute-start | bytes 884744 | tf_op jit(solution)/shard_map/ppermute | solution.py:15
  223.3 128.3 %collective-permute-start.3 = (f32[16,1,6,768]{3,0,2,1:T(8,128)}, f32[16,1,6,768]{3,0,2,1:T(8,128)}, u32[]{:S(2)}, u32[]{:S(2)}) collective-permute-start(f32[16,1,6,768]{3,0,2,1:T(8,128)} %get-tuple-element.14), channel_id=1, source_target_pairs={{1,0},{2,1},{3,2},{4,3},{5,4},{6,5},{7,6},{8,7},{9,8},{10,9},{11,1... | collective-permute-start | bytes 884744 | tf_op jit(solution)/shard_map/ppermute | solution.py:17
  339.7 1.0 copy-start.3
  413.6 120.9 %collective-permute-start.4 = (f32[16,1,6,768]{3,0,2,1:T(8,128)}, f32[16,1,6,768]{3,0,2,1:T(8,128)}, u32[]{:S(2)}, u32[]{:S(2)}) collective-permute-start(f32[16,1,6,768]{3,0,2,1:T(8,128)} %get-tuple-element.5), channel_id=1, source_target_pairs={{0,1},{1,2},{2,3},{3,4},{4,5},{5,6},{6,7},{7,8},{8,9},{9,10},{10,1... | collective-permute-start | bytes 884744 | tf_op jit(solution)/shard_map/ppermute | solution.py:15
  416.8 117.7 %collective-permute-start.5 = (f32[16,1,6,768]{3,0,2,1:T(8,128)}, f32[16,1,6,768]{3,0,2,1:T(8,128)}, u32[]{:S(2)}, u32[]{:S(2)}) collective-permute-start(f32[16,1,6,768]{3,0,2,1:T(8,128)} %get-tuple-element.8), channel_id=1, source_target_pairs={{1,0},{2,1},{3,2},{4,3},{5,4},{6,5},{7,6},{8,7},{9,8},{10,9},{11,1... | collective-permute-start | bytes 884744 | tf_op jit(solution)/shard_map/ppermute | solution.py:17
  524.7 1.0 copy-start.1
  530.5 5.4 copy-start.5
  530.5 5.4 copy-start.6
  534.5 1.5 copy-start
Sparse Core Ops, SparseCore 0:
  38.2 99.5 all-reduce.3
  220.1 96.1 all-reduce.5
  413.7 96.0 all-reduce.7
where the time goes:
time: 606 us; the launch traced here: 597 us
  waiting for transfers between devices  271 us (45%)
  local copies, waits for them, and re-layouts  162 us (27%)
  other arithmetic  126 us (21%)
  starting transfers between devices  15.1 us (2%)
  between operations  13.8 us (2%)
  matrix products  7.85 us (1%)
    psum x3, waiting for transfers between devices, gather_edges(): edge_set = lax.psum(rim_cells, 'ty')  271 us
    add x2, other arithmetic, laplace(): metric[0] * (padded_x[..., :-2] - source)  68.1 us
    add x1, other arithmetic, per_device(): fields - damp_four[:, None, None, None] * fourth  35.3 us
    unnamed x19, local copies, waits for them, and re-layouts  28.6 us
    reshape x5, local copies, waits for them, and re-layouts, seam_halo(): neighbor = neighbor.reshape(levels, 6, 4, row_width)  20.2 us
    slice x4, local copies, waits for them, and re-layouts, strip_edges(): east_cells = jnp.transpose(source[:, :, :, -1], (0, 2, 1))  18.6 us
    add x1, local copies, waits for them, and re-layouts, per_device(): fields - damp_four[:, None, None, None] * fourth  18.5 us
    broadcast_in_dim x6, local copies, waits for them, and re-layouts, laplace(): jnp.transpose(lax.dynamic_slice_in_dim(halo_cells[:, :, 1], row_start, st...  15.9 us
  transfers between devices with their start and end apart: 9, of which 3 were waited for; matrix products, arithmetic and copies ran while one was open for 14% of the time, Pallas kernels for 0%

commit v1 on v0

--- a/solution.py
+++ b/solution.py
@@ -1,7 +1,16 @@
+import functools
 import jax
 import jax.numpy as jnp
 from jax import lax
 from jax.sharding import PartitionSpec as P
+
+
+def lay_the_roads(inp, axis_name):
+    e_next = jax.lax.all_gather(inp, axis_name=axis_name)
+    return jnp.sum(e_next, axis=0)
+
+
+recast_pages = functools.partial(lay_the_roads, axis_name="ty")
 
 
 def with_halo(cells, sides, width):
@@ -38,7 +47,7 @@
     blank = jnp.zeros(strip_cells.shape[:3] + (row_width,), jnp.float32)
     placed = lax.dynamic_update_slice_in_dim(blank, strip_cells, tile_index * strip_rows, 3)
     rim_cells = jnp.stack([first_row, placed[:, :, 0], last_row, placed[:, :, 1]], axis=2)
-    edge_set = lax.psum(rim_cells, "ty")
+    edge_set = recast_pages(rim_cells)
     return edge_set
 
 

time: 606 us -> 649 us (1.071)
  other arithmetic: 126 us -> 163 us
  waiting for transfers between devices: 271 us -> 293 us
  local copies, waits for them, and re-layouts: 162 us -> 146 us
    all_gather x0 -> x3, waiting for transfers between devices: none -> 292 us  [lay_the_roads(): e_next = jax.lax.all_gather(inp, axis_name=axis_name)]
    psum x3 -> x0, waiting for transfers between devices: 271 us -> none  [gather_edges(): edge_set = lax.psum(rim_cells, 'ty')]
    reduce_sum x0 -> x3, other arithmetic: none -> 29.5 us  [lay_the_roads(): return jnp.sum(e_next, axis=0)]
    reshape x5, local copies, waits for them, and re-layouts: 20.2 us -> 12 us  [seam_halo(): neighbor = neighbor.reshape(levels, 6, 4, row_width)]
    reshape x3 -> x0, local copies, waits for them, and re-layouts: 6.85 us -> none  [seam_halo(): flattened = edge_set.reshape(levels, 24, row_width)]
    unnamed x19 -> x21, local copies, waits for them, and re-layouts: 28.6 us -> 28.6 us
  transfers between devices with their start and end apart: 9 -> 9, of which waited for: 3 -> 3; matrix products, arithmetic and copies ran while one was open for 14% -> 17% of each run, Pallas kernels for 0% -> 0%
where the time goes in v1:
time: 649 us; the launch traced here: 639 us
  waiting for transfers between devices  293 us (45%)
  other arithmetic  163 us (25%)
  local copies, waits for them, and re-layouts  146 us (22%)
  starting transfers between devices  18.3 us (3%)
  between operations  13.8 us (2%)
    all_gather x3, waiting for transfers between devices, lay_the_roads(): e_next = jax.lax.all_gather(inp, axis_name=axis_name)  292 us
    add x2, other arithmetic, laplace(): metric[0] * (padded_x[..., :-2] - source)  70.8 us
    add x1, other arithmetic, per_device(): fields - damp_four[:, None, None, None] * fourth  35.1 us
    reduce_sum x3, other arithmetic, lay_the_roads(): return jnp.sum(e_next, axis=0)  29.5 us
    unnamed x21, local copies, waits for them, and re-layouts  28.6 us
    slice x4, local copies, waits for them, and re-layouts, strip_edges(): east_cells = jnp.transpose(source[:, :, :, -1], (0, 2, 1))  18.6 us
    add x1, local copies, waits for them, and re-layouts, per_device(): fields - damp_four[:, None, None, None] * fourth  18.5 us
    broadcast_in_dim x6, local copies, waits for them, and re-layouts, laplace(): jnp.transpose(lax.dynamic_slice_in_dim(halo_cells[:, :, 1], row_start, st...  16 us
  transfers between devices with their start and end apart: 9, of which 3 were waited for; matrix products, arithmetic and copies ran while one was open for 17% of the time, Pallas kernels for 0%

profile of v1, /device:TPU:0, one launch (start us, length us, event | category | flops | bytes accessed | tf_op | source)
XLA Modules:
  0.0 639.4 jit_solution(6559607055131979618)
XLA Ops:
  6.5 4.6 fusion.57
  11.1 18.5 %copy.168 = f32[16,48,6,768]{3,0,2,1:T(8,128)} copy(f32[16,48,6,768]{3,1,2,0:T(8,128)} %param.5) | data formatting | bytes 28311552 | tf_op args[0]
  38.7 4.7 collective-permute-start
  48.6 96.5 %all-gather.7.cloned.1.call-done = f32[256,6,4,768]{3,0,1,2:T(8,128)} async-done(((f32[16,6,4,768]{3,0,1,2:T(8,128)}), f32[256,6,4,768]{3,0,1,2:T(8,128)}) %all-gather.7.cloned.1.call-update) | async-done | bytes 18874384 | tf_op jit(solution)/shard_map/all_gather | solution.py:9
  145.1 9.8 %reduce_sum.27 = f32[16,6,4,768]{3,0,1,2:T(8,128)} reduce(f32[16,16,6,4,768]{4,1,0,2,3:T(8,128)} %bitcast.138, f32[]{:T(128)} %constant.20.clone.1), dimensions={0}, to_apply=%region_0.1 | reduce | flops 4423680 | bytes 20054020 | tf_op jit(solution)/shard_map/reduce_sum | solution.py:10
  159.0 5.1 rev.9
  168.4 4.0 copy.146
  174.0 4.0 copy.151
  180.1 35.1 %fusion.26 = f32[16,48,6,768]{3,0,2,1:T(8,128)} fusion(f32[16,48,6,768]{3,0,2,1:T(8,128)} %copy.168, f32[16,1,6,768]{3,0,2,1:T(8,128)} %get-tuple-element.38, f32[16,1,6,768]{3,0,2,1:T(8,128)} %get-tuple-element.37, f32[16,48,6,1]{3,0,2,1:T(8,128)} %copy.151, f32[16,48,6,1]{3,0,2,1:T(8,128)} %copy.146, f32[48,6,768]{2,1,0:T(8,128)} %copy.157, ...), kind=kLoop, calls=%fused_computation.35 | loop fusion | flops 53084160 | bytes 32477184 | tf_op jit(solution)/shard_map/add | solution.py:84
  215.2 5.4 fusion.55
  222.6 3.4 copy.184
  226.0 3.4 copy.161
  236.8 4.6 collective-permute-start.2
  242.7 97.6 %all-gather.9.cloned.1.call-done = f32[256,6,4,768]{3,0,1,2:T(8,128)} async-done(((f32[16,6,4,768]{3,0,1,2:T(8,128)}), f32[256,6,4,768]{3,0,1,2:T(8,128)}) %all-gather.9.cloned.1.call-update) | async-done | bytes 18874384 | tf_op jit(solution)/shard_map/all_gather | solution.py:9
  340.3 9.8 %reduce_sum.28 = f32[16,6,4,768]{3,0,1,2:T(8,128)} reduce(f32[16,16,6,4,768]{4,1,0,2,3:T(8,128)} %bitcast.139, f32[]{:T(128)} %constant.20.clone.1), dimensions={0}, to_apply=%region_1.2 | reduce | flops 4423680 | bytes 20054020 | tf_op jit(solution)/shard_map/reduce_sum | solution.py:10
  353.8 2.7 reshape.133
  359.2 4.7 rev.10
  368.5 4.0 copy.166
  374.0 4.0 copy.167
  380.1 35.7 %fusion.15 = f32[16,48,6,768]{3,0,2,1:T(8,128)} fusion(f32[16,48,6,768]{3,0,2,1:T(8,128)} %fusion.26, f32[16,1,6,768]{3,0,2,1:T(8,128)} %get-tuple-element.34, f32[16,1,6,768]{3,0,2,1:T(8,128)} %get-tuple-element.33, f32[16,48,6,1]{3,0,2,1:T(8,128)} %copy.167, f32[16,48,6,1]{3,0,2,1:T(8,128)} %copy.166, f32[48,6,768]{2,1,0:T(8,128)} %copy.157, ...), kind=kLoop, calls=%fused_computation.20 | loop fusion | flops 53084160 | bytes 32477184 | tf_op jit(solution)/shard_map/add | solution.py:84
  415.8 5.3 fusion.53
  423.3 3.4 copy.169
  426.7 3.4 copy.170
  437.4 4.6 collective-permute-start.4
  443.5 98.4 %all-gather.11.cloned.1.call-done = f32[256,6,4,768]{3,0,1,2:T(8,128)} async-done(((f32[16,6,4,768]{3,0,1,2:T(8,128)}), f32[256,6,4,768]{3,0,1,2:T(8,128)}) %all-gather.11.cloned.1.call-update) | async-done | bytes 18874384 | tf_op jit(solution)/shard_map/all_gather | solution.py:9
  541.9 9.8 %reduce_sum.29 = f32[16,6,4,768]{3,0,1,2:T(8,128)} reduce(f32[16,16,6,4,768]{4,1,0,2,3:T(8,128)} %bitcast.140, f32[]{:T(128)} %constant.20.clone.1), dimensions={0}, to_apply=%region_2.3 | reduce | flops 4423680 | bytes 20054020 | tf_op jit(solution)/shard_map/reduce_sum | solution.py:10
  558.1 2.7 copy.175
  560.8 4.7 rev.11
  569.3 3.9 copy.177
  573.2 4.0 copy.178
  578.8 35.1 %fusion.4 = f32[16,48,6,768]{3,0,2,1:T(8,128)} fusion(f32[16,48,6,768]{3,0,2,1:T(8,128)} %fusion.15, f32[16,1,6,768]{3,0,2,1:T(8,128)S(1)} %get-tuple-element.30, f32[16,1,6,768]{3,0,2,1:T(8,128)S(1)} %get-tuple-element.29, f32[16,48,6,1]{3,0,2,1:T(8,128)} %copy.178, f32[16,48,6,1]{3,0,2,1:T(8,128)} %copy.177, f32[16]{0:T(128)S(1)} %copy-done.6, ...), kind=kLoop, calls=%fused_computation.5 | loop fusion | flops 67239936 | bytes 46633088 | tf_op jit(solution)/shard_map/add | solution.py:95
  613.9 18.5 %copy.179 = f32[16,48,6,768]{3,1,2,0:T(8,128)} copy(f32[16,48,6,768]{3,0,2,1:T(8,128)} %fusion.4) | data formatting | bytes 28311552 | tf_op jit(solution)/shard_map/add | solution.py:95
  (85 shorter events, 74.0 us)
Async XLA Ops:
  6.5 138.5 %all-gather.7.cloned.1.call-start = ((), (), s32[]{:S(2)}) async-start(), calls=%async_computation | async-start | bytes 20054016 | tf_op jit(solution)/shard_map/all_gather | solution.py:9
  34.3 10.6 %copy-start.5 = (s32[6,4,3]{0,1,2:T(4,128)S(1)}, s32[6,4,3]{0,1,2:T(4,128)}, u32[]{:S(2)}) copy-start(s32[6,4,3]{0,1,2:T(4,128)} %param.9) | copy-start | bytes 868
  34.3 10.9 %copy-start.4 = (f32[4,48,6,768]{3,1,2,0:T(8,128)S(1)}, f32[4,48,6,768]{3,1,2,0:T(8,128)}, u32[]{:S(2)}) copy-start(f32[4,48,6,768]{3,1,2,0:T(8,128)} %param.8) | copy-start | bytes 10616836
  38.6 301.7 %all-gather.9.cloned.1.call-start = ((), (), s32[]{:S(2)}) async-start(), calls=%async_computation.1 | async-start | bytes 20054016 | tf_op jit(solution)/shard_map/all_gather | solution.py:9
  38.7 139.4 %collective-permute-start = (f32[16,1,6,768]{3,0,2,1:T(8,128)}, f32[16,1,6,768]{3,0,2,1:T(8,128)}, u32[]{:S(2)}, u32[]{:S(2)}) collective-permute-start(f32[16,1,6,768]{3,0,2,1:T(8,128)} %get-tuple-element.17), channel_id=1, source_target_pairs={{0,1},{1,2},{2,3},{3,4},{4,5},{5,6},{6,7},{7,8},{8,9},{9,10},{10,1... | collective-permute-start | bytes 884744 | tf_op jit(solution)/shard_map/ppermute | solution.py:24
  43.4 134.7 %collective-permute-start.1 = (f32[16,1,6,768]{3,0,2,1:T(8,128)}, f32[16,1,6,768]{3,0,2,1:T(8,128)}, u32[]{:S(2)}, u32[]{:S(2)}) collective-permute-start(f32[16,1,6,768]{3,0,2,1:T(8,128)} %get-tuple-element.19), channel_id=1, source_target_pairs={{1,0},{2,1},{3,2},{4,3},{5,4},{6,5},{7,6},{8,7},{9,8},{10,9},{11,1... | collective-permute-start | bytes 884744 | tf_op jit(solution)/shard_map/ppermute | solution.py:26
  165.9 1.1 copy-start.2
  236.8 305.2 %all-gather.11.cloned.1.call-start = ((), (), s32[]{:S(2)}) async-start(), calls=%async_computation.2 | async-start | bytes 20054016 | tf_op jit(solution)/shard_map/all_gather | solution.py:9
  236.8 141.2 %collective-permute-start.2 = (f32[16,1,6,768]{3,0,2,1:T(8,128)}, f32[16,1,6,768]{3,0,2,1:T(8,128)}, u32[]{:S(2)}, u32[]{:S(2)}) collective-permute-start(f32[16,1,6,768]{3,0,2,1:T(8,128)} %get-tuple-element.11), channel_id=1, source_target_pairs={{0,1},{1,2},{2,3},{3,4},{4,5},{5,6},{6,7},{7,8},{8,9},{9,10},{10,1... | collective-permute-start | bytes 884744 | tf_op jit(solution)/shard_map/ppermute | solution.py:24
  241.4 136.6 %collective-permute-start.3 = (f32[16,1,6,768]{3,0,2,1:T(8,128)}, f32[16,1,6,768]{3,0,2,1:T(8,128)}, u32[]{:S(2)}, u32[]{:S(2)}) collective-permute-start(f32[16,1,6,768]{3,0,2,1:T(8,128)} %get-tuple-element.14), channel_id=1, source_target_pairs={{1,0},{2,1},{3,2},{4,3},{5,4},{6,5},{7,6},{8,7},{9,8},{10,9},{11,1... | collective-permute-start | bytes 884744 | tf_op jit(solution)/shard_map/ppermute | solution.py:26
  366.0 1.0 copy-start.3
  437.4 139.9 %collective-permute-start.4 = (f32[16,1,6,768]{3,0,2,1:T(8,128)}, f32[16,1,6,768]{3,0,2,1:T(8,128)}, u32[]{:S(2)}, u32[]{:S(2)}) collective-permute-start(f32[16,1,6,768]{3,0,2,1:T(8,128)} %get-tuple-element.5), channel_id=1, source_target_pairs={{0,1},{1,2},{2,3},{3,4},{4,5},{5,6},{6,7},{7,8},{8,9},{9,10},{10,1... | collective-permute-start | bytes 884744 | tf_op jit(solution)/shard_map/ppermute | solution.py:24
  442.0 135.3 %collective-permute-start.5 = (f32[16,1,6,768]{3,0,2,1:T(8,128)}, f32[16,1,6,768]{3,0,2,1:T(8,128)}, u32[]{:S(2)}, u32[]{:S(2)}) collective-permute-start(f32[16,1,6,768]{3,0,2,1:T(8,128)} %get-tuple-element.8), channel_id=1, source_target_pairs={{1,0},{2,1},{3,2},{4,3},{5,4},{6,5},{7,6},{8,7},{9,8},{10,9},{11,1... | collective-permute-start | bytes 884744 | tf_op jit(solution)/shard_map/ppermute | solution.py:26
  567.5 1.0 copy-start.1
  573.2 5.3 copy-start.6
  573.2 5.4 copy-start.7
  577.3 1.5 copy-start
Sparse Core Ops, SparseCore 0:
  38.7 106.2 all-gather.6
  236.9 103.3 all-gather.8
  437.5 104.3 all-gather.10
